TPU v7x, 512 devices: a whole 4x4x16 slice. The times are simulated.
512 devices in a mesh: rep: 16 (over x, z_lo), mp: 32 (over z_hi, y, core).
Axes of the slice: x: 4, y: 4, z: 16 (z_hi: 4, z_lo: 4; z = z_hi * 4 + z_lo), core: 2. Of those that a mesh axis runs over, the one named last changes fastest.
Arguments:
- dense_feats: bfloat16 [65536, 13], P(('rep', 'mp')), may hold values from -6 to 6
- bag_counts: int32 [65536, 32, 64], P('rep', 'mp'), may hold values from 0 to 2
- emb_rows: bfloat16 [32, 64, 256], P('mp'), may hold values from -0.625 to 0.625
- v_emb: bfloat16 [8192, 256], P('mp'), may hold values from -0.0625 to 0.0625
- u_emb: bfloat16 [256, 8192], P(None, 'mp'), may hold values from -0.375 to 0.375
- b_emb: bfloat16 [8192], P('mp'), may hold values from -3 to 3
- v_bot: bfloat16 [256, 256], replicated, may hold values from -0.375 to 0.375
- u_bot: bfloat16 [256, 256], replicated, may hold values from -0.375 to 0.375
- b_bot: bfloat16 [256], replicated, may hold values from -3 to 3
- w_first: bfloat16 [13, 1024], replicated, may hold values from -1.75 to 1.75
- b_first: bfloat16 [1024], replicated, may hold values from -3 to 3
- w_second: bfloat16 [1024, 256], replicated, may hold values from -0.1875 to 0.1875
- b_second: bfloat16 [256], replicated, may hold values from -3 to 3
- cot_cross: bfloat16 [65536, 8192], P(('rep', 'mp')), may hold values from -24 to 24
- cot_bottom: bfloat16 [65536, 256], P(('rep', 'mp')), may hold values from -6 to 6
Outputs:
- cross_emb: bfloat16 [65536, 8192], P(('rep', 'mp'))
- cross_bot: bfloat16 [65536, 256], P(('rep', 'mp'))
- grad_table: bfloat16 [32, 64, 256], P('mp')
- grad_v_emb: bfloat16 [8192, 256], P('mp')
- grad_u_emb: bfloat16 [256, 8192], P(None, 'mp')
- grad_b_emb: bfloat16 [8192], P('mp')
- grad_v_bot: bfloat16 [256, 256], replicated
- grad_u_bot: bfloat16 [256, 256], replicated
- grad_b_bot: bfloat16 [256], replicated
- grad_w_first: bfloat16 [13, 1024], replicated
- grad_b_first: bfloat16 [1024], replicated
- grad_w_second: bfloat16 [1024, 256], replicated
- grad_b_second: bfloat16 [256], replicated
Inputs may be any that keep to these rules, and one draw needn't show every extreme that they name: bag_counts[s, t, j] is how often row j of table t occurs in the bag of sample s.
All inputs are finite; a program needn't handle non-finite values.
Results may differ from a plain program's by a relative error of at most 0.029.
Values may be sent and summed in bfloat16 or wider, within the bound.
A program may use at most 64 MiB of HBM per device.

v0:
```python
import math
import jax
import jax.numpy as jnp
from jax import lax
from jax.sharding import PartitionSpec as P


def silu_slope(inputs):
    gate_value = jax.nn.sigmoid(inputs)
    return gate_value * (1.0 + inputs * (1.0 - gate_value))


def contract_rows(left_side, right_side):
    return lax.dot_general(
        left_side, right_side, (((0,), (0,)), ((), ())), preferred_element_type=jnp.float32
    )


def contract_cols(left_side, right_side):
    return lax.dot_general(
        left_side, right_side, (((1,), (1,)), ((), ())), preferred_element_type=jnp.float32
    )


def local(
    dense_feats,
    bag_counts,
    emb_rows,
    v_emb,
    u_emb,
    b_emb,
    v_bot,
    u_bot,
    b_bot,
    w_first,
    b_first,
    w_second,
    b_second,
    cot_cross,
    cot_bottom,
):
    tables = lax.axis_size("mp")
    replicas = lax.axis_size("rep")
    own_rows = dense_feats.shape[0]
    table_rows, width = emb_rows.shape[1:]
    rank = v_emb.shape[1]
    share = width // replicas
    grad_scale = 1.0 / math.sqrt(own_rows * tables * replicas)
    first = lax.axis_index("rep") * share
    pad = -(table_rows + 1) % 128
    packed = jnp.concatenate(
        [v_emb, u_emb.T, emb_rows[0].T, b_emb[:, None], jnp.zeros((width, pad), jnp.bfloat16)],
        axis=1,
    )
    packed = lax.dynamic_slice_in_dim(packed, first, share, 0)
    columns = packed.shape[1]
    packed = lax.all_gather(packed, "mp", axis=0, tiled=True)
    packed = lax.all_gather(packed, "rep", axis=0, tiled=True)
    packed = jnp.swapaxes(packed.reshape(replicas, tables, share, columns), 0, 1)
    packed = packed.reshape(tables * width, columns)
    counts = bag_counts[:, 0, :].astype(jnp.bfloat16)
    counts = jnp.swapaxes(counts.reshape(tables, own_rows, table_rows), 1, 2)
    counts = lax.all_to_all(counts, "mp", split_axis=0, concat_axis=0, tiled=True)
    first_pre = jnp.dot(dense_feats, w_first, preferred_element_type=jnp.float32) + b_first.astype(
        jnp.float32
    )
    first_act = jax.nn.silu(first_pre).astype(jnp.bfloat16)
    second_pre = jnp.dot(first_act, w_second, preferred_element_type=jnp.float32) + b_second.astype(
        jnp.float32
    )
    bottom = jax.nn.silu(second_pre).astype(jnp.bfloat16)
    v_all = packed[:, :rank]
    u_all = packed[:, rank : 2 * rank]
    emb_all = packed[:, 2 * rank : 2 * rank + table_rows].reshape(tables, width, table_rows)
    b_all = packed[:, 2 * rank + table_rows].reshape(1, tables * width).astype(jnp.float32)
    pooled = lax.dot_general(
        counts, emb_all, (((1,), (2,)), ((0,), (0,))), preferred_element_type=jnp.float32
    ).astype(jnp.bfloat16)
    pooled = jnp.swapaxes(pooled, 0, 1).reshape(own_rows, tables * width)
    low_rank = (
        jnp.dot(pooled, v_all, preferred_element_type=jnp.float32)
        + jnp.dot(bottom, v_bot, preferred_element_type=jnp.float32)
    ).astype(jnp.bfloat16)
    lift_emb = contract_cols(low_rank, u_all) + b_all
    pooled_full = pooled.astype(jnp.float32)
    cross_emb = (pooled_full * (lift_emb + 1.0)).astype(jnp.bfloat16)
    lift_bottom = jnp.dot(low_rank, u_bot, preferred_element_type=jnp.float32) + b_bot.astype(
        jnp.float32
    )
    bottom_full = bottom.astype(jnp.float32)
    cross_bot = (bottom_full * (lift_bottom + 1.0)).astype(jnp.bfloat16)
    cot_rows = cot_cross.astype(jnp.float32)
    d_lift = cot_rows * pooled_full
    d_lift_round = d_lift.astype(jnp.bfloat16)
    cot_low = cot_bottom.astype(jnp.float32)
    d_bottom_lift = cot_low * bottom_full
    d_bottom_round = d_bottom_lift.astype(jnp.bfloat16)
    d_low = (
        jnp.dot(d_lift_round, u_all, preferred_element_type=jnp.float32)
        + contract_cols(d_bottom_round, u_bot)
    ).astype(jnp.bfloat16)
    d_pooled = (cot_rows * (lift_emb + 1.0) + contract_cols(d_low, v_all)).astype(jnp.bfloat16)
    d_tables = jnp.swapaxes(d_pooled.reshape(own_rows, tables, width), 0, 1)
    grad_table = lax.dot_general(
        d_tables, counts, (((1,), (2,)), ((0,), (0,))), preferred_element_type=jnp.float32
    ).reshape(tables * width, table_rows)
    grad_v = contract_rows(pooled, d_low)
    grad_u = contract_rows(d_lift_round, low_rank)
    grad_b = jnp.sum(d_lift, axis=0)
    grads = jnp.concatenate(
        [
            grad_v.astype(jnp.bfloat16),
            grad_u.astype(jnp.bfloat16),
            grad_table.astype(jnp.bfloat16),
            grad_b.astype(jnp.bfloat16)[:, None],
            jnp.zeros((tables * width, pad), jnp.bfloat16),
        ],
        axis=1,
    )
    d_bottom = cot_low * (lift_bottom + 1.0) + contract_cols(d_low, v_bot)
    grad_vb = grad_scale * contract_rows(bottom, d_low)
    grad_ub = grad_scale * contract_rows(low_rank, d_bottom_round)
    grad_bb = grad_scale * jnp.sum(d_bottom_lift, axis=0)
    d_second = d_bottom * silu_slope(second_pre)
    d_second_round = d_second.astype(jnp.bfloat16)
    grad_ws = grad_scale * contract_rows(first_act, d_second_round)
    grad_bs = grad_scale * jnp.sum(d_second, axis=0)
    d_first = contract_cols(d_second_round, w_second) * silu_slope(first_pre)
    d_first_round = d_first.astype(jnp.bfloat16)
    grad_wf = grad_scale * contract_rows(dense_feats, d_first_round)
    grad_bf = grad_scale * jnp.sum(d_first, axis=0)
    grads = jnp.swapaxes(grads.reshape(tables, replicas, share, columns), 0, 1)
    grads = grads.reshape(replicas * tables * share, columns)
    dense = (grad_wf, grad_bf, grad_ws, grad_bs, grad_vb, grad_ub, grad_bb)
    grads, dense = lax.optimization_barrier((grads, dense))
    grads = lax.psum_scatter(grads, "rep", scatter_dimension=0, tiled=True)
    dense_sums = lax.psum(dense, ("rep", "mp"))
    grads, dense_sums = lax.optimization_barrier((grads, dense_sums))
    grads = lax.psum_scatter(
        grads.astype(jnp.float32) * grad_scale, "mp", scatter_dimension=0, tiled=True
    )
    grads = lax.optimization_barrier(grads).astype(jnp.bfloat16)
    grads = lax.all_gather(grads, "rep", axis=0, tiled=True)
    return (
        cross_emb,
        cross_bot,
        grads[:, 2 * rank : 2 * rank + table_rows].T[None],
        grads[:, :rank],
        grads[:, rank : 2 * rank].T,
        grads[:, 2 * rank + table_rows],
        dense_sums[4].astype(jnp.bfloat16),
        dense_sums[5].astype(jnp.bfloat16),
        dense_sums[6].astype(jnp.bfloat16),
        dense_sums[0].astype(jnp.bfloat16),
        dense_sums[1].astype(jnp.bfloat16),
        dense_sums[2].astype(jnp.bfloat16),
        dense_sums[3].astype(jnp.bfloat16),
    )


def solution(mesh):
    return jax.shard_map(
        local,
        mesh=mesh,
        in_specs=(
            P(("rep", "mp"), None),
            P("rep", "mp", None),
            P("mp", None, None),
            P("mp", None),
            P(None, "mp"),
            P("mp"),
            P(),
            P(),
            P(),
            P(),
            P(),
            P(),
            P(),
            P(("rep", "mp"), None),
            P(("rep", "mp"), None),
        ),
        out_specs=(
            P(("rep", "mp"), None),
            P(("rep", "mp"), None),
            P("mp", None, None),
            P("mp", None),
            P(None, "mp"),
            P("mp"),
            P(),
            P(),
            P(),
            P(),
            P(),
            P(),
            P(),
        ),
        check_vma=False,
    )
```

profile of v0, /device:TPU:8, one launch (start us, length us, event | category | flops | bytes accessed | tf_op | source)
XLA Modules:
  0.0 810.7 jit_solution(15563284094259363290)
XLA Ops:
  7.3 1.1 copy.49
  10.1 1.0 concatenate.11
  11.2 57.4 %all_gather.9 = bf16[512,640]{1,0:T(8,128)(2,1)} all-gather(bf16[16,640]{1,0:T(8,128)(2,1)S(1)} %constant_dynamic-slice_fusion), channel_id=1, replica_groups=mesh['rep'=16,'mp'=32] {'mp'}, dimensions={0}, use_global_device_ids=true | all-gather | bytes 675840 | tf_op jit(solution)/shard_map/all_gather | solution.py:57
  68.5 1.3 convert_bitcast_fusion
  71.0 12.9 %all-to-all-start = ((bf16[32,64,128]{2,1,0:T(8,128)(2,1)}), bf16[32,64,128]{2,1,0:T(8,128)(2,1)S(1)}, u32[]{:S(2)}, u32[]{:S(2)}) async-start(bf16[32,64,128]{2,1,0:T(8,128)(2,1)} %bitcast.72), calls=%async_computation | async-start | bytes 1048576 | tf_op jit(solution)/shard_map/all_to_all | solution.py:63
  86.0 237.6 %all-gather.2.cloned.1.call-done = bf16[8192,640]{1,0:T(8,128)(2,1)} async-done(((bf16[512,640]{1,0:T(8,128)(2,1)}), bf16[8192,640]{1,0:T(8,128)(2,1)}) %all-gather.2.cloned.1.call-update) | async-done | bytes 10485776 | tf_op jit(solution)/shard_map/all_gather | solution.py:58
  323.5 9.6 %copy.52 = bf16[32,16,16,640]{3,2,1,0:T(8,128)(2,1)} copy(bf16[32,16,16,640]{3,2,0,1:T(8,128)(2,1)} %bitcast.87) | data formatting | bytes 20971520 | tf_op jit(solution)/shard_map/transpose | solution.py:59
  333.2 1.7 slice.32
  335.6 1.3 copy-done.4
  336.9 3.1 fusion.9
  340.0 3.1 copy.56
  343.1 3.0 convert_reduce_fusion
  346.2 3.7 fusion.5
  350.1 3.4 convolution_convert_fusion
  353.8 3.3 convolution_convert_fusion.1
  358.2 1.1 fusion.29
  359.3 1.4 convolution_multiply_fusion
  361.8 3.0 fusion.3
  364.8 1.5 fusion.1
  366.8 1.8 copy.58
  368.6 2.1 copy.61
  370.9 4.2 copy.62
  375.1 4.8 copy.60
  379.9 2.5 copy.59
  382.6 1.7 broadcast_in_dim.18
  384.3 18.8 %concatenate.14 = bf16[32,16,16,640]{3,2,0,1:T(8,128)(2,1)} concatenate(bf16[32,16,16,256]{3,2,0,1:T(8,128)(2,1)} %copy.59, bf16[32,16,16,256]{3,2,0,1:T(8,128)(2,1)} %copy.60, bf16[32,16,16,64]{3,2,0,1:T(8,128)(2,1)S(1)} %copy.61, bf16[32,16,16,1]{3,2,0,1:T(8,128)(2,1)} %copy.62, bf16[32,16,16,63]{3,2,0,1:T(8,128)(2,1)} %broadcast_in_dim.18), dimensions={3} | concatenate | bytes 20971520 | tf_op jit(solution)/shard_map/concatenate | solution.py:110
  403.2 1.1 copy-done.6
  404.4 125.4 %all-reduce.2 = (bf16[13,1024]{1,0:T(8,128)(2,1)}, bf16[1024]{0:T(1024)(128)(2,1)}, bf16[1024,256]{1,0:T(8,128)(2,1)}, bf16[256]{0:T(256)(128)(2,1)}, bf16[256,2...) all-reduce(f32[13,1024]{1,0:T(8,128)S(1)} %fusion.18, ...), channel_id=1, replica_groups=mesh['rep'=16,'mp'=32] {'rep','mp'}, use_global_device_ids=true, to_apply=%region_5.6 | all-reduce | flops 408064 | bytes 2448384 | tf_op jit(solution)/shard_map/psum | solution.py:137
  529.8 109.0 %reduce-scatter.3.cloned.1.call-done = bf16[512,640]{1,0:T(8,128)(2,1)} async-done(((bf16[8192,640]{1,0:T(8,128)(2,1)}), bf16[512,640]{1,0:T(8,128)(2,1)}) %reduce-scatter.3.cloned.1.call-update) | async-done | bytes 655376 | tf_op jit(solution)/shard_map/reduce_scatter | solution.py:136
  638.8 2.3 convert_multiply_fusion.3
  641.1 115.5 %reduce-scatter.5.cloned.1.call-done = f32[16,640]{1,0:T(8,128)} async-done(((f32[512,640]{1,0:T(8,128)}), f32[16,640]{1,0:T(8,128)}) %reduce-scatter.5.cloned.1.call-update) | async-done | bytes 40976 | tf_op jit(solution)/shard_map/reduce_scatter | solution.py:139
  757.3 44.0 %all_gather.11 = bf16[256,640]{1,0:T(8,128)(2,1)S(1)} all-gather(bf16[16,640]{1,0:T(8,128)(2,1)S(1)} %convert_element_type.164), channel_id=1, replica_groups=mesh['rep'=16,'mp'=32] {'rep'}, dimensions={0}, use_global_device_ids=true | all-gather | bytes 348160 | tf_op jit(solution)/shard_map/all_gather | solution.py:143
  (81 shorter events, 12.6 us)
Async XLA Ops:
  7.2 77.8 %copy-start = (bf16[1024,256]{1,0:T(8,128)(2,1)S(1)}, bf16[1024,256]{1,0:T(8,128)(2,1)}, u32[]{:S(2)}) copy-start(bf16[1024,256]{1,0:T(8,128)(2,1)} %param.26) | copy-start | bytes 1572868
  7.2 76.7 %copy-start.16 = (bf16[1024]{0:T(1024)(128)(2,1)S(1)}, bf16[1024]{0:T(1024)(128)(2,1)}, u32[]{:S(2)}) copy-start(bf16[1024]{0:T(1024)(128)(2,1)} %param.25) | copy-start | bytes 6148
  7.2 76.7 %copy-start.17 = (bf16[256]{0:T(256)(128)(2,1)S(1)}, bf16[256]{0:T(256)(128)(2,1)}, u32[]{:S(2)}) copy-start(bf16[256]{0:T(256)(128)(2,1)} %param.27) | copy-start | bytes 1540
  7.2 76.7 %copy-start.18 = (bf16[256]{0:T(256)(128)(2,1)S(1)}, bf16[256]{0:T(256)(128)(2,1)}, u32[]{:S(2)}) copy-start(bf16[256]{0:T(256)(128)(2,1)} %param.23) | copy-start | bytes 1540
  7.2 76.7 %copy-start.15 = (bf16[128,13]{0,1:T(8,128)(2,1)S(1)}, bf16[128,13]{0,1:T(8,128)(2,1)}, u32[]{:S(2)}) copy-start(bf16[128,13]{0,1:T(8,128)(2,1)} %param.15) | copy-start | bytes 9988
  7.2 76.7 %copy-start.14 = (bf16[13,1024]{1,0:T(8,128)(2,1)S(1)}, bf16[13,1024]{1,0:T(8,128)(2,1)}, u32[]{:S(2)}) copy-start(bf16[13,1024]{1,0:T(8,128)(2,1)} %param.24) | copy-start | bytes 79876
  7.2 77.8 %copy-start.11 = (bf16[128,256]{1,0:T(8,128)(2,1)S(1)}, bf16[128,256]{1,0:T(8,128)(2,1)}, u32[]{:S(2)}) copy-start(bf16[128,256]{1,0:T(8,128)(2,1)} %param.29) | copy-start | bytes 196612
  7.3 316.3 %all-gather.2.cloned.1.call-start = ((), (), s32[]{:S(2)}) async-start(), calls=%async_computation.3 | async-start | bytes 11141120 | tf_op jit(solution)/shard_map/all_gather | solution.py:58
  71.0 263.9 %all-to-all-start = ((bf16[32,64,128]{2,1,0:T(8,128)(2,1)}), bf16[32,64,128]{2,1,0:T(8,128)(2,1)S(1)}, u32[]{:S(2)}, u32[]{:S(2)}) async-start(bf16[32,64,128]{2,1,0:T(8,128)(2,1)} %bitcast.72), calls=%async_computation | async-start | bytes 1048576 | tf_op jit(solution)/shard_map/all_to_all | solution.py:63
  83.8 554.9 %reduce-scatter.3.cloned.1.call-start = ((), (), s32[]{:S(2)}) async-start(), calls=%async_computation.4 | async-start | bytes 11141120 | tf_op jit(solution)/shard_map/reduce_scatter | solution.py:136
  84.2 0.8 copy-start.9
  335.6 1.3 copy-start.4
  346.1 3.8 copy-start.13
  346.1 3.9 copy-start.2
  350.1 3.5 copy-start.8
  350.1 3.7 copy-start.5
  350.1 11.7 %slice-start = ((s8[10485760]{0:T(1024)(128)(4,1)}), s8[4194304]{0:T(1024)(128)(4,1)S(1)}, s32[]{:S(2)}) async-start(s8[10485760]{0:T(1024)(128)(4,1)} %bitcast.77), calls=%async_computation.6 | async-start | bytes 8388608
  350.1 11.7 %slice-start.1 = ((s8[10485760]{0:T(1024)(128)(4,1)}), s8[4194304]{0:T(1024)(128)(4,1)S(1)}, s32[]{:S(2)}) async-start(s8[10485760]{0:T(1024)(128)(4,1)} %bitcast.77), calls=%async_computation.7 | async-start | bytes 8388608
  353.8 4.1 copy-start.19
  353.8 4.4 copy-start.10
  353.8 8.0 slice-start.2
  375.1 4.8 copy-start.3
  379.9 2.5 copy-start.12
  403.1 1.2 copy-start.6
  403.1 1.3 copy-start.7
  403.2 401.0 %copy-start.1 = (bf16[1024,256]{1,0:T(8,128)(2,1)S(1)}, bf16[1024,256]{1,0:T(8,128)(2,1)}, u32[]{:S(2)}) copy-start(bf16[1024,256]{1,0:T(8,128)(2,1)} %param.26) | copy-start | bytes 1572868
  403.2 353.4 %reduce-scatter.5.cloned.1.call-start = ((), (), s32[]{:S(2)}) async-start(), calls=%async_computation.5 | async-start | bytes 1351680 | tf_op jit(solution)/shard_map/reduce_scatter | solution.py:139
Sparse Core Ops, SparseCore 0:
  68.7 254.8 all-gather.1
  403.3 235.4 reduce-scatter.2
  643.2 113.3 reduce-scatter.4
where the time goes:
time: 812 us; the launch traced here: 811 us
  waiting for transfers between devices  462 us (57%)
  blocking collectives  227 us (28%)
  local copies, waits for them, and re-layouts  61.7 us (8%)
  matrix products  25.6 us (3%)
  between operations  14.2 us (2%)
  starting transfers between devices  13 us (2%)
    all_gather x1, waiting for transfers between devices, local(): packed = lax.all_gather(packed, 'rep', axis=0, tiled=True)  238 us
    psum x1, blocking collectives, local(): dense_sums = lax.psum(dense, ('rep', 'mp'))  125 us
    reduce_scatter x1, waiting for transfers between devices, local(): lax.psum_scatter(grads.astype(jnp.float32) * grad_scale, 'mp', scatter_di...  115 us
    reduce_scatter x1, waiting for transfers between devices, local(): grads = lax.psum_scatter(grads, 'rep', scatter_dimension=0, tiled=True)  109 us
    all_gather x1, blocking collectives, local(): packed = lax.all_gather(packed, 'mp', axis=0, tiled=True)  57.4 us
    all_gather x1, blocking collectives, local(): grads = lax.all_gather(grads, 'rep', axis=0, tiled=True)  44 us
    concatenate x3, local copies, waits for them, and re-layouts, local(): jnp.concatenate([grad_v.astype(jnp.bfloat16), grad_u.astype(jnp.bfloat16)...  26.2 us
  transfers between devices with their start and end apart: 4, of which 3 were waited for; matrix products, arithmetic and copies ran while one was open for 2% of the time, Pallas kernels for 0%

commit v1 on v0

--- a/solution.py
+++ b/solution.py
@@ -134,7 +134,9 @@
     dense = (grad_wf, grad_bf, grad_ws, grad_bs, grad_vb, grad_ub, grad_bb)
     grads, dense = lax.optimization_barrier((grads, dense))
     grads = lax.psum_scatter(grads, "rep", scatter_dimension=0, tiled=True)
-    dense_sums = lax.psum(dense, ("rep", "mp"))
+    dense_sums = dense
+    for over in ("rep", "mp"):
+        dense_sums = lax.psum(dense_sums, over)
     grads, dense_sums = lax.optimization_barrier((grads, dense_sums))
     grads = lax.psum_scatter(
         grads.astype(jnp.float32) * grad_scale, "mp", scatter_dimension=0, tiled=True

time: 812 us -> 1060 us (1.31)
  blocking collectives: 227 us -> 388 us
  waiting for transfers between devices: 462 us -> 546 us
    psum x1 -> x2, blocking collectives: 125 us -> 286 us  [local(): dense_sums = lax.psum(dense_sums, over)]
    psum x0 -> x1, waiting for transfers between devices: none -> 99.6 us  [local(): dense_sums = lax.psum(dense_sums, over)]
    reduce_scatter x1, waiting for transfers between devices: 109 us -> 30.4 us  [local(): grads = lax.psum_scatter(grads, 'rep', scatter_dimension=0, tiled=True)]
    reduce_scatter x1, waiting for transfers between devices: 115 us -> 177 us  [local(): lax.psum_scatter(grads.astype(jnp.float32) * grad_scale, 'mp', scatter_di...]
  transfers between devices with their start and end apart: 4 -> 5, of which waited for: 3 -> 4; matrix products, arithmetic and copies ran while one was open for 2% -> 1% of each run, Pallas kernels for 0% -> 0%
where the time goes in v1:
time: 1060 us
  waiting for transfers between devices  546 us (52%)
  blocking collectives  388 us (37%)
  local copies, waits for them, and re-layouts  60.3 us (6%)
  matrix products  32.1 us (3%)
  between operations  14.2 us (1%)
  starting transfers between devices  13 us (1%)
    psum x2, blocking collectives, local(): dense_sums = lax.psum(dense_sums, over)  286 us
    all_gather x1, waiting for transfers between devices, local(): packed = lax.all_gather(packed, 'rep', axis=0, tiled=True)  238 us
    reduce_scatter x1, waiting for transfers between devices, local(): lax.psum_scatter(grads.astype(jnp.float32) * grad_scale, 'mp', scatter_di...  177 us
    psum x1, waiting for transfers between devices, local(): dense_sums = lax.psum(dense_sums, over)  99.6 us
    all_gather x1, blocking collectives, local(): packed = lax.all_gather(packed, 'mp', axis=0, tiled=True)  57.4 us
    all_gather x1, blocking collectives, local(): grads = lax.all_gather(grads, 'rep', axis=0, tiled=True)  44.1 us
    reduce_scatter x1, waiting for transfers between devices, local(): grads = lax.psum_scatter(grads, 'rep', scatter_dimension=0, tiled=True)  30.4 us
    concatenate x3, local copies, waits for them, and re-layouts, local(): jnp.concatenate([grad_v.astype(jnp.bfloat16), grad_u.astype(jnp.bfloat16)...  26.2 us
  transfers between devices with their start and end apart: 5, of which 4 were waited for; matrix products, arithmetic and copies ran while one was open for 1% of the time, Pallas kernels for 0%

profile of v1, /device:TPU:8, one launch (start us, length us, event | category | flops | bytes accessed | tf_op | source)
XLA Modules:
  0.0 1060.4 jit_solution(10795764540435657977)
XLA Ops:
  7.3 1.1 copy.49
  11.2 57.4 %all_gather.9 = bf16[512,640]{1,0:T(8,128)(2,1)} all-gather(bf16[16,640]{1,0:T(8,128)(2,1)S(1)} %constant_dynamic-slice_fusion), channel_id=1, replica_groups=mesh['rep'=16,'mp'=32] {'mp'}, dimensions={0}, use_global_device_ids=true | all-gather | bytes 675840 | tf_op jit(solution)/shard_map/all_gather | solution.py:57
  68.5 1.3 convert_bitcast_fusion
  71.0 12.9 %all-to-all-start = ((bf16[32,64,128]{2,1,0:T(8,128)(2,1)}), bf16[32,64,128]{2,1,0:T(8,128)(2,1)S(1)}, u32[]{:S(2)}, u32[]{:S(2)}) async-start(bf16[32,64,128]{2,1,0:T(8,128)(2,1)} %bitcast.72), calls=%async_computation | async-start | bytes 1048576 | tf_op jit(solution)/shard_map/all_to_all | solution.py:63
  86.0 237.6 %all-gather.2.cloned.1.call-done = bf16[8192,640]{1,0:T(8,128)(2,1)} async-done(((bf16[512,640]{1,0:T(8,128)(2,1)}), bf16[8192,640]{1,0:T(8,128)(2,1)}) %all-gather.2.cloned.1.call-update) | async-done | bytes 10485776 | tf_op jit(solution)/shard_map/all_gather | solution.py:58
  323.5 9.6 copy.52
  333.1 1.7 slice.32
  335.6 1.3 copy-done.5
  336.9 3.8 fusion.9
  340.7 2.9 copy.56
  343.6 3.0 convert_reduce_fusion
  346.6 3.7 fusion.5
  350.6 3.3 convolution_convert_fusion
  354.1 3.3 convolution_convert_fusion.1
  358.4 1.1 fusion.29
  359.5 1.4 convolution_multiply_fusion
  362.7 6.0 fusion.3
  368.7 3.8 fusion.1
  373.0 1.8 copy.58
  374.8 2.1 copy.61
  377.1 4.2 copy.62
  381.3 4.8 copy.60
  386.1 2.5 copy.59
  388.7 1.7 broadcast_in_dim.18
  390.4 18.8 %concatenate.14 = bf16[32,16,16,640]{3,2,0,1:T(8,128)(2,1)} concatenate(bf16[32,16,16,256]{3,2,0,1:T(8,128)(2,1)} %copy.59, bf16[32,16,16,256]{3,2,0,1:T(8,128)(2,1)} %copy.60, bf16[32,16,16,64]{3,2,0,1:T(8,128)(2,1)S(1)} %copy.61, bf16[32,16,16,1]{3,2,0,1:T(8,128)(2,1)} %copy.62, bf16[32,16,16,63]{3,2,0,1:T(8,128)(2,1)} %broadcast_in_dim.18), dimensions={3} | concatenate | bytes 20971520 | tf_op jit(solution)/shard_map/concatenate | solution.py:110
  410.1 79.9 %all-reduce.1 = (f32[13,1024]{1,0:T(8,128)S(1)}, f32[1024]{0:T(1024)S(1)}, f32[256]{0:T(256)S(1)}, f32[256]{0:T(256)S(1)}) all-reduce(f32[13,1024]{1,0:T(8,128)S(1)} %fusion.18, f32[1024]{0:T(1024)S(1)} %broadcast_multiply_fusion, f32[256]{0:T(256)S(1)} %get-tuple-element.33, ...), channel_id=1, replica_groups=mesh['rep'=16,'mp'=32] {'rep'}, use_global_device_ids=true, to_apply=%region_5.6 | all-reduce | flops 14848 | bytes 118784 | tf_op jit(solution)/shard_map/psum | solution.py:139
  490.0 99.6 %all-reduce.6.cloned.1.call-done = (f32[1024,256]{1,0:T(8,128)}, f32[256,256]{1,0:T(8,128)}, f32[256,256]{1,0:T(8,128)}) async-done(((f32[1024,256]{1,0:T(8,128)}, f32[256,256]{1,0:T(8,128)}, f32[256,256]{1,0:T(8,128)}), (f32[1024,256]{1,0:T(8,128)}, f32[256,256]{1,0:T(8,128)}, f32[256,256]{1,0:T(8,128)})) %all-reduce.6.cloned.1.call-update) | async-done | bytes 1572880 | tf_op jit(solution)/shard_map/psum | solution.py:139
  589.6 206.5 %all-reduce.7 = (bf16[13,1024]{1,0:T(8,128)(2,1)}, bf16[1024]{0:T(1024)(128)(2,1)}, bf16[1024,256]{1,0:T(8,128)(2,1)}, bf16[256]{0:T(256)(128)(2,1)}, bf16[256,2...) all-reduce(f32[13,1024]{1,0:T(8,128)S(1)} %get-tuple-element.91, ...), channel_id=1, replica_groups=mesh['rep'=16,'mp'=32] {'mp'}, use_global_device_ids=true, to_apply=%region_6.7 | all-reduce | flops 408064 | bytes 2448384 | tf_op jit(solution)/shard_map/psum | solution.py:139
  796.1 30.4 %reduce-scatter.3.cloned.1.call-done = bf16[512,640]{1,0:T(8,128)(2,1)} async-done(((bf16[8192,640]{1,0:T(8,128)(2,1)}), bf16[512,640]{1,0:T(8,128)(2,1)}) %reduce-scatter.3.cloned.1.call-update) | async-done | bytes 655376 | tf_op jit(solution)/shard_map/reduce_scatter | solution.py:136
  826.4 2.3 convert_multiply_fusion.3
  828.7 177.4 %reduce-scatter.5.cloned.1.call-done = f32[16,640]{1,0:T(8,128)} async-done(((f32[512,640]{1,0:T(8,128)}), f32[16,640]{1,0:T(8,128)}) %reduce-scatter.5.cloned.1.call-update) | async-done | bytes 40976 | tf_op jit(solution)/shard_map/reduce_scatter | solution.py:141
  1006.9 44.1 %all_gather.11 = bf16[256,640]{1,0:T(8,128)(2,1)S(1)} all-gather(bf16[16,640]{1,0:T(8,128)(2,1)S(1)} %convert_element_type.164), channel_id=1, replica_groups=mesh['rep'=16,'mp'=32] {'rep'}, dimensions={0}, use_global_device_ids=true | all-gather | bytes 348160 | tf_op jit(solution)/shard_map/all_gather | solution.py:145
  (78 shorter events, 15.1 us)
Async XLA Ops:
  7.2 77.8 %copy-start = (bf16[1024,256]{1,0:T(8,128)(2,1)S(1)}, bf16[1024,256]{1,0:T(8,128)(2,1)}, u32[]{:S(2)}) copy-start(bf16[1024,256]{1,0:T(8,128)(2,1)} %param.26) | copy-start | bytes 1572868
  7.2 76.7 %copy-start.16 = (bf16[1024]{0:T(1024)(128)(2,1)S(1)}, bf16[1024]{0:T(1024)(128)(2,1)}, u32[]{:S(2)}) copy-start(bf16[1024]{0:T(1024)(128)(2,1)} %param.25) | copy-start | bytes 6148
  7.2 76.7 %copy-start.17 = (bf16[256]{0:T(256)(128)(2,1)S(1)}, bf16[256]{0:T(256)(128)(2,1)}, u32[]{:S(2)}) copy-start(bf16[256]{0:T(256)(128)(2,1)} %param.27) | copy-start | bytes 1540
  7.2 76.7 %copy-start.18 = (bf16[256]{0:T(256)(128)(2,1)S(1)}, bf16[256]{0:T(256)(128)(2,1)}, u32[]{:S(2)}) copy-start(bf16[256]{0:T(256)(128)(2,1)} %param.23) | copy-start | bytes 1540
  7.2 76.7 %copy-start.15 = (bf16[128,13]{0,1:T(8,128)(2,1)S(1)}, bf16[128,13]{0,1:T(8,128)(2,1)}, u32[]{:S(2)}) copy-start(bf16[128,13]{0,1:T(8,128)(2,1)} %param.15) | copy-start | bytes 9988
  7.2 76.7 %copy-start.14 = (bf16[13,1024]{1,0:T(8,128)(2,1)S(1)}, bf16[13,1024]{1,0:T(8,128)(2,1)}, u32[]{:S(2)}) copy-start(bf16[13,1024]{1,0:T(8,128)(2,1)} %param.24) | copy-start | bytes 79876
  7.2 77.8 %copy-start.10 = (bf16[128,256]{1,0:T(8,128)(2,1)S(1)}, bf16[128,256]{1,0:T(8,128)(2,1)}, u32[]{:S(2)}) copy-start(bf16[128,256]{1,0:T(8,128)(2,1)} %param.29) | copy-start | bytes 196612
  7.3 316.3 %all-gather.2.cloned.1.call-start = ((), (), s32[]{:S(2)}) async-start(), calls=%async_computation.3 | async-start | bytes 11141120 | tf_op jit(solution)/shard_map/all_gather | solution.py:58
  71.0 263.9 %all-to-all-start = ((bf16[32,64,128]{2,1,0:T(8,128)(2,1)}), bf16[32,64,128]{2,1,0:T(8,128)(2,1)S(1)}, u32[]{:S(2)}, u32[]{:S(2)}) async-start(bf16[32,64,128]{2,1,0:T(8,128)(2,1)} %bitcast.72), calls=%async_computation | async-start | bytes 1048576 | tf_op jit(solution)/shard_map/all_to_all | solution.py:63
  83.8 505.8 %all-reduce.6.cloned.1.call-start = ((), (), s32[]{:S(2)}) async-start(), calls=%async_computation.6 | async-start | bytes 3145728 | tf_op jit(solution)/shard_map/psum | solution.py:139
  84.2 0.8 copy-start.8
  335.6 1.3 copy-start.5
  346.6 3.8 copy-start.12
  346.6 3.8 copy-start.13
  346.6 3.9 copy-start.2
  350.6 3.3 copy-start.7
  350.6 3.5 copy-start.6
  354.1 4.1 copy-start.19
  354.1 4.3 copy-start.9
  362.7 6.0 copy-start.3
  381.3 4.8 copy-start.4
  386.1 2.5 copy-start.11
  409.3 417.1 %reduce-scatter.3.cloned.1.call-start = ((), (), s32[]{:S(2)}) async-start(), calls=%async_computation.4 | async-start | bytes 11141120 | tf_op jit(solution)/shard_map/reduce_scatter | solution.py:136
  410.1 643.8 %copy-start.1 = (bf16[1024,256]{1,0:T(8,128)(2,1)S(1)}, bf16[1024,256]{1,0:T(8,128)(2,1)}, u32[]{:S(2)}) copy-start(bf16[1024,256]{1,0:T(8,128)(2,1)} %param.26) | copy-start | bytes 1572868
  410.1 596.0 %reduce-scatter.5.cloned.1.call-start = ((), (), s32[]{:S(2)}) async-start(), calls=%async_computation.5 | async-start | bytes 1351680 | tf_op jit(solution)/shard_map/reduce_scatter | solution.py:141
Sparse Core Ops, SparseCore 0:
  68.7 254.8 all-gather.1
  409.4 180.1 all-reduce.5
  592.7 233.6 reduce-scatter.2
  831.3 174.7 reduce-scatter.4
